TPU v7x, 32 devices: a whole 2x2x4 slice. The times are simulated.
32 devices in a mesh: replica: 4 (over y, x), fsdp: 2 (over core), tensor: 4 (over z).
Axes of the slice: x: 2, y: 2, z: 4, core: 2. Of those that a mesh axis runs over, the one named last changes fastest.
Arguments:
- attn_out: bfloat16 [2048, 8192], P(('replica', 'tensor'), 'fsdp'), may hold values from -6 to 6
- out_grad: bfloat16 [2048, 8192], P(('replica', 'fsdp'), 'tensor'), may hold values from -0.25 to 0.25
- error_in: float32 [4, 8192, 8192], P('replica', 'fsdp', 'tensor'), may hold values from -4 to 4
- factor_in: float32 [8192, 32], P('tensor'), may hold values from -0.0625 to 0.0625
Outputs:
- new_error: float32 [4, 8192, 8192], P('replica', 'fsdp', 'tensor')
- update: bfloat16 [8192, 8192], P('fsdp', 'tensor')
- new_factor: float32 [8192, 32], P('tensor')
All inputs are finite; a program needn't handle non-finite values.
Results may differ from a plain program's by a relative error of at most 0.001.
Values may be sent and summed in bfloat16 or wider, within the bound.
A program may use at most 128 MiB of HBM per device.

v0:
```python
import jax
import jax.numpy as jnp
from jax import lax
from jax.sharding import PartitionSpec as P


def fold_rows(out_grad, activations, memory):
    return memory + lax.dot_general(
        activations,
        lax.all_gather(out_grad, "fsdp", axis=0, tiled=True),
        (((0,), (0,)), ((), ())),
        preferred_element_type=jnp.float32,
    )


def orthonormalize(partial_left, replicas):
    left = lax.psum(partial_left, ("replica", "tensor")) / replicas
    gram_local = jnp.dot(left.T, left, precision=lax.Precision.HIGHEST)
    gram_matrix = lax.psum(gram_local, "fsdp")
    triangle = jnp.linalg.cholesky(gram_matrix)
    return jax.scipy.linalg.solve_triangular(triangle, left.T, lower=True).T


def body(attn_out, out_grad, error_in, factor_in):
    activations = lax.all_gather(attn_out, "tensor", axis=0, tiled=True)
    replicas = lax.axis_size("replica")
    projected = jnp.dot(out_grad.astype(jnp.float32), factor_in, precision=lax.Precision.HIGHEST)
    projected_all = lax.all_gather(projected, "fsdp", axis=0, tiled=True)
    partial_left = lax.dot_general(
        activations,
        projected_all,
        (((0,), (0,)), ((), ())),
        precision=lax.Precision.HIGHEST,
        preferred_element_type=jnp.float32,
    )
    partial_left = partial_left + jnp.dot(error_in[0], factor_in, precision=lax.Precision.HIGHEST)
    orthonormal = orthonormalize(partial_left, replicas)
    merged = fold_rows(out_grad, activations, error_in[0])
    factor_local = lax.dot_general(
        merged, orthonormal, (((0,), (0,)), ((), ())), precision=lax.Precision.HIGHEST
    )
    new_factor = lax.psum(factor_local, ("replica", "fsdp")) / replicas
    decompressed = jnp.dot(orthonormal, new_factor.T, precision=lax.Precision.HIGHEST)
    new_error = (merged - decompressed)[None]
    return (new_error, decompressed.astype(jnp.bfloat16), new_factor)


def solution(mesh):
    placed = (
        P(("replica", "tensor"), "fsdp"),
        P(("replica", "fsdp"), "tensor"),
        P("replica", "fsdp", "tensor"),
        P("tensor", None),
    )
    return jax.shard_map(
        body,
        mesh=mesh,
        in_specs=placed,
        out_specs=(P("replica", "fsdp", "tensor"), P("fsdp", "tensor"), P("tensor", None)),
        check_vma=False,
    )
```

profile of v0, /device:TPU:0, one launch (start us, length us, event | category | flops | bytes accessed | tf_op | source)
XLA Modules:
  0.0 355.7 jit_solution(17522907834601763414)
XLA Ops:
  7.2 0.0 copy-start
  7.2 0.0 all-gather.3.cloned.1.call-start
  7.2 0.7 all-gather.3.cloned.1.call-update
  7.9 0.0 all-gather.5.cloned.1.call-start
  8.0 0.7 all-gather.5.cloned.1.call-update
  8.7 0.0 all-reduce.3.cloned.1.call-start
  8.7 0.0 copy-done
  8.7 2.2 fusion.15
  10.9 2.1 all_gather.11
  13.0 34.1 %fusion = f32[4096,32]{0,1:T(8,128)S(1)} fusion(f32[2048,32]{0,1:T(8,128)S(1)} %copy-done, f32[1,4096,2048]{2,1,0:T(8,128)} %param.6), kind=kOutput, calls=%fused_computation | convolution fusion | flops 3221225472 | bytes 34340864 | tf_op jit(solution)/shard_map/dot_general | solution.py:36
  47.2 45.9 %all-gather.3.cloned.1.call-done = bf16[512,4096]{1,0:T(8,128)(2,1)} async-done(((bf16[128,4096]{1,0:T(8,128)(2,1)}), bf16[512,4096]{1,0:T(8,128)(2,1)}) %all-gather.3.cloned.1.call-update) | async-done | bytes 4194320 | tf_op jit(solution)/shard_map/all_gather | solution.py:25
  93.1 5.2 %fusion.2 = f32[4096,32]{0,1:T(8,128)} fusion(f32[4096,32]{0,1:T(8,128)S(1)} %fusion, f32[512,32]{1,0:T(8,128)S(1)} %all_gather.11, bf16[512,4096]{1,0:T(8,128)(2,1)} %all-gather.3.cloned.1.call-done), kind=kOutput, calls=%fused_computation.5 | convolution fusion | flops 805437440 | bytes 5308416 | tf_op jit(solution)/shard_map/dot_general | solution.py:29
  98.3 0.0 all-reduce.3.cloned.1.call-update
  98.3 0.2 all-reduce.5.cloned.1.call-start
  98.5 5.2 %all-gather.5.cloned.1.call-done = bf16[512,2048]{1,0:T(8,128)(2,1)} async-done(((bf16[256,2048]{1,0:T(8,128)(2,1)}), bf16[512,2048]{1,0:T(8,128)(2,1)}) %all-gather.5.cloned.1.call-update) | async-done | bytes 2097168 | tf_op jit(solution)/shard_map/all_gather | solution.py:10
  103.7 28.3 %bitcast_add_fusion = f32[4096,2048]{1,0:T(8,128)} fusion(f32[1,4096,2048]{2,1,0:T(8,128)} %param.6, bf16[512,4096]{1,0:T(8,128)(2,1)} %all-gather.3.cloned.1.call-done, bf16[512,2048]{1,0:T(8,128)(2,1)} %all-gather.5.cloned.1.call-done), kind=kOutput, calls=%fused_computation.2 | convolution fusion | flops 8598323200 | bytes 73400320 | tf_op jit(solution)/shard_map/dot_general | solution.py:8
  132.0 87.7 %all-reduce.3.cloned.1.call-done = f32[4096,32]{0,1:T(8,128)} async-done(((f32[4096,32]{0,1:T(8,128)}), f32[4096,32]{0,1:T(8,128)}) %all-reduce.3.cloned.1.call-update) | async-done | bytes 524304 | tf_op jit(solution)/shard_map/psum | solution.py:17
  219.7 1.8 fusion.5
  221.6 3.4 psum.22
  224.9 0.1 copy.8
  225.0 2.9 cholesky.16
  228.0 0.6 compare_reduce_fusion
  228.6 0.7 fusion.9
  229.3 2.4 custom-call.7
  231.7 1.7 fusion.3
  233.4 24.4 %fusion.16 = f32[2048,32]{0,1:T(8,128)} fusion(f32[4096,2048]{1,0:T(8,128)} %bitcast_add_fusion, f32[32,4096]{1,0:T(8,128)S(1)} %fusion.3), kind=kOutput, calls=%fused_computation.26 | convolution fusion | flops 3221225472 | bytes 34340864 | tf_op jit(solution)/shard_map/dot_general | solution.py:39
  257.8 0.0 all-reduce.5.cloned.1.call-update
  257.8 53.0 %all-reduce.5.cloned.1.call-done = f32[2048,32]{0,1:T(8,128)} async-done(((f32[2048,32]{0,1:T(8,128)}), f32[2048,32]{0,1:T(8,128)}) %all-reduce.5.cloned.1.call-update) | async-done | bytes 262160 | tf_op jit(solution)/shard_map/psum | solution.py:42
  310.8 1.0 broadcast_multiply_fusion
  311.9 0.0 copy-start.2
  311.9 37.2 %fusion.14 = (bf16[4096,2048]{1,0:T(8,128)(2,1)}, f32[1,4096,2048]{2,1,0:T(8,128)}) fusion(f32[4096,2048]{1,0:T(8,128)} %bitcast_add_fusion, f32[32,4096]{1,0:T(8,128)S(1)} %fusion.3, f32[2048,32]{0,1:T(8,128)S(1)} %broadcast_multiply_fusion), kind=kOutput, calls=%fused_computation.24 | convolution fusion | flops 3238002688 | bytes 84672512 | tf_op jit(solution)/shard_map/dot_general | solution.py:43
  349.1 0.0 copy-done.2
  (4 shorter events, 0.0 us)
Async XLA Ops:
  7.2 1.5 copy-start
  7.2 85.9 %all-gather.3.cloned.1.call-start = ((), (), s32[]{:S(2)}) async-start(), calls=%async_computation | async-start | bytes 5242880 | tf_op jit(solution)/shard_map/all_gather | solution.py:25
  7.9 95.8 %all-gather.5.cloned.1.call-start = ((), (), s32[]{:S(2)}) async-start(), calls=%async_computation.1 | async-start | bytes 3145728 | tf_op jit(solution)/shard_map/all_gather | solution.py:10
  8.7 211.1 %all-reduce.3.cloned.1.call-start = ((), (), s32[]{:S(2)}) async-start(), calls=%async_computation.2 | async-start | bytes 1048576 | tf_op jit(solution)/shard_map/psum | solution.py:17
  98.3 212.5 %all-reduce.5.cloned.1.call-start = ((), (), s32[]{:S(2)}) async-start(), calls=%async_computation.3 | async-start | bytes 524288 | tf_op jit(solution)/shard_map/psum | solution.py:42
  310.8 38.3 %copy-start.1 = (f32[2048,32]{0,1:T(8,128)S(1)}, f32[2048,32]{0,1:T(8,128)}, u32[]{:S(2)}) copy-start(f32[2048,32]{0,1:T(8,128)} %param.7) | copy-start | bytes 786436
  311.9 37.3 %copy-start.2 = (f32[2048,32]{0,1:T(8,128)}, f32[2048,32]{0,1:T(8,128)S(1)}, u32[]{:S(2)}) copy-start(f32[2048,32]{0,1:T(8,128)S(1)} %broadcast_multiply_fusion) | copy-start | bytes 786436
Sparse Core Ops, SparseCore 0:
  9.6 83.4 all-gather.2
  94.6 9.0 all-gather.4
  109.4 110.2 all-reduce.2
  257.9 52.8 all-reduce.4
where the time goes:
time: 356 us
  waiting for transfers between devices  193 us (54%)
  matrix products  135 us (38%)
  between operations  13.8 us (4%)
  other arithmetic  7.7 us (2%)
  blocking collectives  5.48 us (2%)
    psum x1, waiting for transfers between devices, orthonormalize(): left = lax.psum(partial_left, ('replica', 'tensor')) / replicas  87.7 us
    psum x1, waiting for transfers between devices, body(): new_factor = lax.psum(factor_local, ('replica', 'fsdp')) / replicas  53 us
    all_gather x1, waiting for transfers between devices, body(): activations = lax.all_gather(attn_out, 'tensor', axis=0, tiled=True)  45.9 us
    dot_general x1, matrix products, body(): jnp.dot(orthonormal, new_factor.T, precision=lax.Precision.HIGHEST)  37.2 us
    dot_general x1, matrix products, body(): jnp.dot(error_in[0], factor_in, precision=lax.Precision.HIGHEST)  34.1 us
    dot_general x1, matrix products, fold_rows(): lax.dot_general(activations, lax.all_gather(out_grad, 'fsdp', axis=0, til...  28.3 us
    dot_general x1, matrix products, body(): lax.dot_general(merged, orthonormal, (((0,), (0,)), ((), ())), precision=...  24.4 us
  transfers between devices with their start and end apart: 4, of which 4 were waited for; matrix products, arithmetic and copies ran while one was open for 20% of the time, Pallas kernels for 0%

commit v1 on v0

--- a/solution.py
+++ b/solution.py
@@ -22,7 +22,14 @@
 
 
 def body(attn_out, out_grad, error_in, factor_in):
-    activations = lax.all_gather(attn_out, "tensor", axis=0, tiled=True)
+    ring = [attn_out]
+    for hop in range(3):
+        ring.append(lax.ppermute(ring[-1], "tensor", [(dev, (dev + 1) % 4) for dev in range(4)]))
+    activations = jnp.roll(
+        jnp.concatenate(ring[::-1], axis=0),
+        (lax.axis_index("tensor") + 1) * ring[0].shape[0],
+        axis=0,
+    )
     replicas = lax.axis_size("replica")
     projected = jnp.dot(out_grad.astype(jnp.float32), factor_in, precision=lax.Precision.HIGHEST)
     projected_all = lax.all_gather(projected, "fsdp", axis=0, tiled=True)

time: 356 us -> 350 us (0.983)
  waiting for transfers between devices: 193 us -> 181 us
  local copies, waits for them, and re-layouts: 0.1 us -> 4.16 us
    ppermute x0 -> x3, waiting for transfers between devices: none -> 47.1 us  [body(): lax.ppermute(ring[-1], 'tensor', [(dev, (dev + 1) % 4) for dev in range(4)])]
    all_gather x1 -> x0, waiting for transfers between devices: 45.9 us -> none  [body(): activations = lax.all_gather(attn_out, 'tensor', axis=0, tiled=True)]
    psum x1, waiting for transfers between devices: 87.7 us -> 81.1 us  [orthonormalize(): left = lax.psum(partial_left, ('replica', 'tensor')) / replicas]
    all_gather x1, waiting for transfers between devices: 5.16 us -> 0.02 us  [fold_rows(): lax.all_gather(out_grad, 'fsdp', axis=0, tiled=True)]
    unnamed x6 -> x19, local copies, waits for them, and re-layouts: 0.02 us -> 4.02 us
  transfers between devices with their start and end apart: 4 -> 6, of which waited for: 4 -> 4; matrix products, arithmetic and copies ran while one was open for 20% -> 20% of each run, Pallas kernels for 0% -> 0%
where the time goes in v1:
time: 350 us
  waiting for transfers between devices  181 us (52%)
  matrix products  133 us (38%)
  between operations  15.7 us (4%)
  other arithmetic  7.66 us (2%)
  blocking collectives  5.49 us (2%)
  local copies, waits for them, and re-layouts  4.16 us (1%)
    psum x1, waiting for transfers between devices, orthonormalize(): left = lax.psum(partial_left, ('replica', 'tensor')) / replicas  81.1 us
    psum x1, waiting for transfers between devices, body(): new_factor = lax.psum(factor_local, ('replica', 'fsdp')) / replicas  52.5 us
    ppermute x3, waiting for transfers between devices, body(): lax.ppermute(ring[-1], 'tensor', [(dev, (dev + 1) % 4) for dev in range(4)])  47.1 us
    dot_general x1, matrix products, body(): jnp.dot(orthonormal, new_factor.T, precision=lax.Precision.HIGHEST)  37.3 us
    dot_general x1, matrix products, body(): jnp.dot(error_in[0], factor_in, precision=lax.Precision.HIGHEST)  34.1 us
    dot_general x1, matrix products, fold_rows(): lax.dot_general(activations, lax.all_gather(out_grad, 'fsdp', axis=0, til...  28.4 us
    dot_general x1, matrix products, body(): lax.dot_general(merged, orthonormal, (((0,), (0,)), ((), ())), precision=...  24.4 us
  transfers between devices with their start and end apart: 6, of which 4 were waited for; matrix products, arithmetic and copies ran while one was open for 20% of the time, Pallas kernels for 0%

profile of v1, /device:TPU:0, one launch (start us, length us, event | category | flops | bytes accessed | tf_op | source)
XLA Modules:
  0.0 350.1 jit_solution(3396239112371096186)
XLA Ops:
  8.1 3.1 collective-permute-start
  11.2 25.4 %collective-permute-done = bf16[128,4096]{1,0:T(8,128)(2,1)S(1)} collective-permute-done((bf16[128,4096]{1,0:T(8,128)(2,1)}, bf16[128,4096]{1,0:T(8,128)(2,1)S(1)}, u32[]{:S(2)}, u32[]{:S(2)}) %collective-permute-start) | collective-permute-done | bytes 1048608 | tf_op jit(solution)/shard_map/ppermute | solution.py:27
  36.6 0.0 all-reduce.3.cloned.1.call-start
  36.7 2.2 fusion.18
  38.9 2.1 all_gather.7
  41.0 21.7 %collective-permute-done.1 = bf16[128,4096]{1,0:T(8,128)(2,1)S(1)} collective-permute-done((bf16[128,4096]{1,0:T(8,128)(2,1)S(1)}, bf16[128,4096]{1,0:T(8,128)(2,1)S(1)}, u32[]{:S(2)}, u32[]{:S(2)}) %collective-permute-start.1) | collective-permute-done | bytes 1048608 | tf_op jit(solution)/shard_map/ppermute | solution.py:27
  62.7 34.1 %fusion = f32[4096,32]{0,1:T(8,128)S(1)} fusion(f32[2048,32]{0,1:T(8,128)S(1)} %copy-done, f32[1,4096,2048]{2,1,0:T(8,128)} %param.6), kind=kOutput, calls=%fused_computation | convolution fusion | flops 3221225472 | bytes 34340864 | tf_op jit(solution)/shard_map/dot_general | solution.py:43
  96.9 0.1 constant_dynamic-update-slice_fusion.7
  97.0 0.1 constant_dynamic-update-slice_fusion.6
  97.0 0.1 constant_dynamic-update-slice_fusion.5
  97.2 0.1 constant_dynamic-update-slice_fusion.4
  97.2 0.1 constant_dynamic-update-slice_fusion.3
  97.3 0.1 constant_dynamic-update-slice_fusion.2
  97.4 0.1 constant_dynamic-update-slice_fusion.1
  97.5 0.1 constant_dynamic-update-slice_fusion
  97.6 3.4 copy-done.2
  101.0 3.1 convolution_add_fusion
  104.1 0.2 all-reduce.5.cloned.1.call-start
  104.4 28.4 %bitcast_add_fusion = f32[4096,2048]{1,0:T(8,128)} fusion(f32[1,4096,2048]{2,1,0:T(8,128)} %param.6, bf16[512,2048]{1,0:T(8,128)(2,1)} %all-gather.2.cloned.1.call-done, bf16[1024,4096]{1,0:T(8,128)(2,1)} %copy-done.2, s32[]{:T(128)S(6)} %select_n.18), kind=kOutput, calls=%fused_computation.2 | convolution fusion | flops 8598323200 | bytes 73400320 | tf_op jit(solution)/shard_map/dot_general | solution.py:8
  132.8 81.1 %all-reduce.3.cloned.1.call-done = f32[4096,32]{0,1:T(8,128)} async-done(((f32[4096,32]{0,1:T(8,128)}), f32[4096,32]{0,1:T(8,128)}) %all-reduce.3.cloned.1.call-update) | async-done | bytes 524304 | tf_op jit(solution)/shard_map/psum | solution.py:17
  213.8 1.8 fusion.6
  215.6 3.4 psum.22
  219.0 0.1 copy.8
  219.1 2.9 cholesky.16
  222.0 0.6 compare_reduce_fusion
  222.7 0.7 fusion.10
  223.3 2.4 custom-call.7
  225.8 1.7 fusion.4
  227.4 24.4 %fusion.19 = f32[2048,32]{0,1:T(8,128)} fusion(f32[4096,2048]{1,0:T(8,128)} %bitcast_add_fusion, f32[32,4096]{1,0:T(8,128)S(1)} %fusion.4), kind=kOutput, calls=%fused_computation.37 | convolution fusion | flops 3221225472 | bytes 34340864 | tf_op jit(solution)/shard_map/dot_general | solution.py:46
  251.9 52.5 %all-reduce.5.cloned.1.call-done = f32[2048,32]{0,1:T(8,128)} async-done(((f32[2048,32]{0,1:T(8,128)}), f32[2048,32]{0,1:T(8,128)}) %all-reduce.5.cloned.1.call-update) | async-done | bytes 262160 | tf_op jit(solution)/shard_map/psum | solution.py:49
  304.4 1.0 broadcast_multiply_fusion
  305.4 37.3 %fusion.17 = (bf16[4096,2048]{1,0:T(8,128)(2,1)}, f32[1,4096,2048]{2,1,0:T(8,128)}) fusion(f32[4096,2048]{1,0:T(8,128)} %bitcast_add_fusion, f32[32,4096]{1,0:T(8,128)S(1)} %fusion.4, f32[2048,32]{0,1:T(8,128)S(1)} %broadcast_multiply_fusion), kind=kOutput, calls=%fused_computation.35 | convolution fusion | flops 3238002688 | bytes 84672512 | tf_op jit(solution)/shard_map/dot_general | solution.py:50
  (21 shorter events, 0.2 us)
Async XLA Ops:
  8.0 28.7 %copy-start = (f32[2048,32]{0,1:T(8,128)S(1)}, f32[2048,32]{0,1:T(8,128)}, u32[]{:S(2)}) copy-start(f32[2048,32]{0,1:T(8,128)} %param.7) | copy-start | bytes 786436
  8.0 96.3 %all-gather.2.cloned.1.call-start = ((), (), s32[]{:S(2)}) async-start(), calls=%async_computation | async-start | bytes 3145728 | tf_op jit(solution)/shard_map/all_gather | solution.py:10
  8.1 28.5 %collective-permute-start = (bf16[128,4096]{1,0:T(8,128)(2,1)}, bf16[128,4096]{1,0:T(8,128)(2,1)S(1)}, u32[]{:S(2)}, u32[]{:S(2)}) collective-permute-start(bf16[128,4096]{1,0:T(8,128)(2,1)} %param.4), channel_id=1, source_target_pairs={{0,1},{1,2},{2,3},{3,0},{4,5},{5,6},{6,7},{7,4},{8,9},{9,10},{10,1... | collective-permute-start | bytes 3145736 | tf_op jit(solution)/shard_map/ppermute | solution.py:27
  36.6 26.1 %collective-permute-start.1 = (bf16[128,4096]{1,0:T(8,128)(2,1)S(1)}, bf16[128,4096]{1,0:T(8,128)(2,1)S(1)}, u32[]{:S(2)}, u32[]{:S(2)}) collective-permute-start(bf16[128,4096]{1,0:T(8,128)(2,1)S(1)} %collective-permute-done), channel_id=1, source_target_pairs={{0,1},{1,2},{2,3},{3,0},{4,5},{5,6},{6,7},{7,4},{8,9},{9,10},{10,1... | collective-permute-start | bytes 3145736 | tf_op jit(solution)/shard_map/ppermute | solution.py:27
  36.6 177.2 %all-reduce.3.cloned.1.call-start = ((), (), s32[]{:S(2)}) async-start(), calls=%async_computation.1 | async-start | bytes 1048576 | tf_op jit(solution)/shard_map/psum | solution.py:17
  41.0 56.2 %copy-start.3 = (bf16[128,4096]{1,0:T(8,128)(2,1)S(1)}, bf16[128,4096]{1,0:T(8,128)(2,1)}, u32[]{:S(2)}) copy-start(bf16[128,4096]{1,0:T(8,128)(2,1)} %param.4) | copy-start | bytes 3145732
  62.7 34.2 %collective-permute-start.2 = (bf16[128,4096]{1,0:T(8,128)(2,1)S(1)}, bf16[128,4096]{1,0:T(8,128)(2,1)S(1)}, u32[]{:S(2)}, u32[]{:S(2)}) collective-permute-start(bf16[128,4096]{1,0:T(8,128)(2,1)S(1)} %collective-permute-done.1), channel_id=1, source_target_pairs={{0,1},{1,2},{2,3},{3,0},{4,5},{5,6},{6,7},{7,4},{8,9},{9,10},{10,1... | collective-permute-start | bytes 3145736 | tf_op jit(solution)/shard_map/ppermute | solution.py:27
  96.8 4.2 %copy-start.5 = (f32[512,32]{1,0:T(8,128)S(1)}, f32[512,32]{1,0:T(8,128)}, u32[]{:S(2)}) copy-start(f32[512,32]{1,0:T(8,128)} %all_gather.7) | copy-start | bytes 196612
  97.6 3.4 copy-start.2
  104.1 200.3 %all-reduce.5.cloned.1.call-start = ((), (), s32[]{:S(2)}) async-start(), calls=%async_computation.2 | async-start | bytes 524288 | tf_op jit(solution)/shard_map/psum | solution.py:49
  305.3 37.3 %copy-start.4 = (f32[2048,32]{0,1:T(8,128)}, f32[2048,32]{0,1:T(8,128)S(1)}, u32[]{:S(2)}) copy-start(f32[2048,32]{0,1:T(8,128)S(1)} %broadcast_multiply_fusion) | copy-start | bytes 786436
  305.4 37.3 %copy-start.1 = (f32[2048,32]{0,1:T(8,128)S(1)}, f32[2048,32]{0,1:T(8,128)}, u32[]{:S(2)}) copy-start(f32[2048,32]{0,1:T(8,128)} %param.7) | copy-start | bytes 786436
Sparse Core Ops, SparseCore 0:
  36.7 12.0 all-gather.1
Sparse Core Ops, SparseCore 1:
  104.2 109.6 all-reduce.2
  252.0 52.4 all-reduce.4
